TPU v7x, 32 devices: a whole 2x2x4 slice. The times are simulated.
32 devices in a mesh: wide: 8 (over y, x, core), narrow: 4 (over z).
Axes of the slice: x: 2, y: 2, z: 4, core: 2. Of those that a mesh axis runs over, the one named last changes fastest.
Arguments:
- tokens: bfloat16 [32768, 768], P(('wide', 'narrow')), may hold values from -6 to 6
- out_grad: bfloat16 [32768, 768], P(('wide', 'narrow')), may hold values from -6 to 6
- routes: int32 [32768, 2], P(('wide', 'narrow')), may hold values from 0 to 15, all different within a row; in each aligned block of 1024 rows (0 to 1023, 1024 to 2047, ...) at most 160 rows name the same one
- replay: int32 [32768], P(('wide', 'narrow')), may hold values 0 or 1
- ln1_gain: bfloat16 [768], P(('wide', 'narrow')), may hold values from 0.5 to 1.5
- ln1_bias: bfloat16 [768], P(('wide', 'narrow')), may hold values from -1.75 to 1.75
- w_qkv: bfloat16 [768, 2304], P(('wide', 'narrow')), may hold values from -0.21875 to 0.21875
- w_out: bfloat16 [768, 768], P(('wide', 'narrow')), may hold values from -3 to 3
- ln2_gain: bfloat16 [768], P(('wide', 'narrow')), may hold values from 0.5 to 1.5
- ln2_bias: bfloat16 [768], P(('wide', 'narrow')), may hold values from -0.625 to 0.625
- w_router: bfloat16 [768, 16], P(('wide', 'narrow')), may hold values from -0.15625 to 0.15625
- frozen_in: bfloat16 [8, 768, 3072], P('wide', 'narrow'), may hold values from -0.21875 to 0.21875
- frozen_out: bfloat16 [8, 3072, 768], P('wide', 'narrow'), may hold values from -0.109375 to 0.109375
- new_in: bfloat16 [8, 768, 3072], P('wide', 'narrow'), may hold values from -0.21875 to 0.21875
- new_out: bfloat16 [8, 3072, 768], P('wide', 'narrow'), may hold values from -0.109375 to 0.109375
Outputs:
- block_out: bfloat16 [32768, 768], P(('wide', 'narrow'))
- tokens_grad: float32 [32768, 768], P(('wide', 'narrow'))
- ln1_gain_grad: float32 [768], P(('wide', 'narrow'))
- ln1_bias_grad: float32 [768], P(('wide', 'narrow'))
- w_qkv_grad: float32 [768, 2304], P(('wide', 'narrow'))
- w_out_grad: float32 [768, 768], P(('wide', 'narrow'))
- ln2_gain_grad: float32 [768], P(('wide', 'narrow'))
- ln2_bias_grad: float32 [768], P(('wide', 'narrow'))
- w_router_grad: float32 [768, 16], P(('wide', 'narrow'))
- new_in_grad: float32 [8, 768, 3072], P('wide', 'narrow')
- new_out_grad: float32 [8, 3072, 768], P('wide', 'narrow')
Inputs may be any that keep to these rules, and one draw needn't show every extreme that they name: `routes`: the two ids of a row differ. In the rows of one device (aligned blocks of 1024 rows) no expert is named more than 160 times, a bound that some block reaches.
All inputs are finite; a program needn't handle non-finite values. No bound on the sum of `replay` on one device may be relied on, other than what follows from the above.
Results may differ from a plain program's by a relative error of at most 0.017.
Values may be sent and summed in bfloat16 or wider, within the bound.
No kernel may reach another device: no remote copies, remote signals or barrier semaphores. Data moves between devices by JAX's collectives and lax.ppermute only.
A program may use at most 192 MiB of HBM per device.

v0:
```python
import jax
import jax.numpy as jnp
from jax import lax
from jax.sharding import PartitionSpec as P

HEADS = 12
HD = 64
SEQ = 1024


EPSILON = 1e-05
SHIFT = 1.0
NEGATIVE = -1e30


def smooth(values):
    return jax.nn.gelu(values, approximate=True)


def layer_norm(values, gain, bias):
    centered = values - jnp.mean(values, axis=-1, keepdims=True)
    inv_std = lax.rsqrt(jnp.mean(centered * centered, axis=-1, keepdims=True) + EPSILON)
    normed = centered * inv_std
    return (normed * gain + bias, normed, inv_std)


def norm_back(grad_norm, normed, inv_std, gain):
    scaled = grad_norm * gain
    return inv_std * (
        scaled
        - jnp.mean(scaled, axis=-1, keepdims=True)
        - normed * jnp.mean(scaled * normed, axis=-1, keepdims=True)
    )


def causal(length):
    places = jnp.arange(length, dtype=jnp.int32)
    return places[:, None] >= places[None, :]


def head_columns(seq_block, head_idx):
    model_width = HEADS * HD
    queries = lax.dynamic_slice_in_dim(seq_block, head_idx * HD, HD, 1)
    key_rows = lax.dynamic_slice_in_dim(seq_block, model_width + head_idx * HD, HD, 1)
    value_rows = lax.dynamic_slice_in_dim(seq_block, 2 * model_width + head_idx * HD, HD, 1)
    return (queries, key_rows, value_rows)


def head_scores(queries, key_rows, allowed):
    scores = lax.dot_general(
        queries, key_rows, (((1,), (1,)), ((), ())), preferred_element_type=jnp.float32
    ) * HD ** (-0.5)
    return jnp.where(allowed, scores, NEGATIVE)


def attend_forward(qkv_low):
    model_width = HEADS * HD
    allowed = causal(SEQ)

    def per_sequence(seq_block):

        def per_head(head_idx):
            queries, key_rows, value_rows = head_columns(seq_block, head_idx)
            scores = head_scores(queries, key_rows, allowed)
            row_top = jnp.max(scores, axis=1, keepdims=True)
            exponent = jnp.exp(scores - row_top)
            row_total = jnp.sum(exponent, axis=1, keepdims=True)
            probs_low = (exponent / row_total).astype(jnp.bfloat16)
            mixed = jnp.dot(probs_low, value_rows, preferred_element_type=jnp.float32).astype(
                jnp.bfloat16
            )
            return (mixed, (row_top + jnp.log(row_total))[:, 0])

        mixed, log_total = lax.map(per_head, jnp.arange(HEADS, dtype=jnp.int32))
        return (jnp.transpose(mixed, (1, 0, 2)).reshape(SEQ, model_width), log_total)

    return lax.map(per_sequence, qkv_low.reshape(-1, SEQ, 3 * model_width))


def attend_backward(qkv_low, grad_mixed, log_totals):
    model_width = HEADS * HD
    allowed = causal(SEQ)
    score_scale = HD ** (-0.5)

    def per_sequence(operands):
        seq_block, grad_block, log_seq = operands

        def per_head(head_idx):
            queries, key_rows, value_rows = head_columns(seq_block, head_idx)
            grad_head = lax.dynamic_slice_in_dim(grad_block, head_idx * HD, HD, 1)
            log_head = lax.dynamic_index_in_dim(log_seq, head_idx, 0, keepdims=False)
            scores = head_scores(queries, key_rows, allowed)
            probs = jnp.exp(scores - log_head[:, None])
            probs_low = probs.astype(jnp.bfloat16)
            grad_probs = lax.dot_general(
                grad_head, value_rows, (((1,), (1,)), ((), ())), preferred_element_type=jnp.float32
            )
            grad_values = lax.dot_general(
                probs_low, grad_head, (((0,), (0,)), ((), ())), preferred_element_type=jnp.float32
            )
            grad_scores = (
                probs * (grad_probs - jnp.sum(probs * grad_probs, axis=1, keepdims=True))
            ).astype(jnp.bfloat16)
            grad_queries = (
                jnp.dot(grad_scores, key_rows, preferred_element_type=jnp.float32) * score_scale
            )
            grad_keys = (
                lax.dot_general(
                    grad_scores,
                    queries,
                    (((0,), (0,)), ((), ())),
                    preferred_element_type=jnp.float32,
                )
                * score_scale
            )
            return jnp.stack([grad_queries, grad_keys, grad_values])

        head_grads = lax.map(per_head, jnp.arange(HEADS, dtype=jnp.int32))
        return (
            jnp.transpose(head_grads, (2, 1, 0, 3))
            .reshape(SEQ, 3 * model_width)
            .astype(jnp.bfloat16)
        )

    operands = (
        qkv_low.reshape(-1, SEQ, 3 * model_width),
        grad_mixed.reshape(-1, SEQ, model_width),
        log_totals,
    )
    return lax.map(per_sequence, operands).reshape(-1, 3 * model_width)


def expert_list(frozen_part, new_part):
    return [frozen_part[0]] + [new_part[0]]


def expert_forward(rows_in, up_weight, down_weight):
    pre_act = jnp.dot(rows_in, up_weight, preferred_element_type=jnp.float32)
    active = smooth(pre_act).astype(jnp.bfloat16)
    return jnp.dot(active, down_weight, preferred_element_type=jnp.float32).astype(jnp.bfloat16)


def expert_backward(rows_in, grad_in, up_weight, down_weight, with_weights):
    pre_act = jnp.dot(rows_in, up_weight, preferred_element_type=jnp.float32)
    active, smooth_back = jax.vjp(smooth, pre_act)
    active_low = active.astype(jnp.bfloat16)
    grad_active = lax.dot_general(
        grad_in, down_weight, (((1,), (1,)), ((), ())), preferred_element_type=jnp.float32
    )
    grad_pre = smooth_back(grad_active)[0].astype(jnp.bfloat16)
    down_grad = None
    up_grad = None
    if with_weights:
        down_grad = lax.dot_general(
            active_low, grad_in, (((0,), (0,)), ((), ())), preferred_element_type=jnp.float32
        )
        up_grad = lax.dot_general(
            rows_in, grad_pre, (((0,), (0,)), ((), ())), preferred_element_type=jnp.float32
        )
    row_grad = lax.dot_general(
        grad_pre, up_weight, (((1,), (1,)), ((), ())), preferred_element_type=jnp.float32
    ).astype(jnp.bfloat16)
    return (active_low, row_grad, down_grad, up_grad)


def local(
    tokens,
    out_grad,
    routes,
    replay,
    ln1_gain,
    ln1_bias,
    w_qkv,
    w_out,
    ln2_gain,
    ln2_bias,
    w_router,
    frozen_in,
    frozen_out,
    new_in,
    new_out,
):
    dense_full = (
        lax.all_gather(ln1_gain, ("wide", "narrow"), axis=0, tiled=True),
        lax.all_gather(ln1_bias, ("wide", "narrow"), axis=0, tiled=True),
        lax.all_gather(w_qkv, ("wide", "narrow"), axis=0, tiled=True),
        lax.all_gather(w_out, ("wide", "narrow"), axis=0, tiled=True),
        lax.all_gather(ln2_gain, ("wide", "narrow"), axis=0, tiled=True),
        lax.all_gather(ln2_bias, ("wide", "narrow"), axis=0, tiled=True),
        lax.all_gather(w_router, ("wide", "narrow"), axis=0, tiled=True),
    )
    expert_full = (
        lax.all_gather(frozen_in, "narrow", axis=1, tiled=True),
        lax.all_gather(frozen_out, "narrow", axis=1, tiled=True),
        lax.all_gather(new_in, "narrow", axis=1, tiled=True),
        lax.all_gather(new_out, "narrow", axis=1, tiled=True),
    )
    frozen_up, frozen_down, new_up, new_down = expert_full
    tok_rows = tokens.shape[0]
    model_width = tokens.shape[1]
    expert_count = w_router.shape[1]
    frozen_local = frozen_up.shape[0]
    group_size = frozen_local + new_up.shape[0]
    capacity = 5 * tok_rows // (2 * expert_count)
    inputs_full = tokens.astype(jnp.float32)
    hidden_one, normed_one, inv_one = layer_norm(
        inputs_full, dense_full[0].astype(jnp.float32), dense_full[1].astype(jnp.float32)
    )
    normed_low = hidden_one.astype(jnp.bfloat16)
    qkv_low = jnp.dot(normed_low, dense_full[2], preferred_element_type=jnp.float32).astype(
        jnp.bfloat16
    )
    mixed_low, log_totals = attend_forward(qkv_low)
    mixed_low = mixed_low.reshape(tok_rows, model_width)
    after_attn = inputs_full + jnp.dot(mixed_low, dense_full[3], preferred_element_type=jnp.float32)
    hidden_two, normed_two, inv_two = layer_norm(
        after_attn, dense_full[4].astype(jnp.float32), dense_full[5].astype(jnp.float32)
    )
    routed_low = hidden_two.astype(jnp.bfloat16)
    logits = jnp.dot(routed_low, dense_full[6], preferred_element_type=jnp.float32)
    expert_ids = jnp.arange(expert_count, dtype=jnp.int32)
    route_hot = (routes[:, :, None] == expert_ids).astype(jnp.float32)
    trainable = (routes % group_size >= frozen_local).astype(jnp.float32)
    picked = (
        jnp.sum(route_hot * logits[:, None, :], axis=2)
        - SHIFT * replay.astype(jnp.float32)[:, None] * trainable
    )
    gates = jax.nn.softmax(picked, axis=1)
    flat_routes = routes.reshape(-1)
    pair_count = flat_routes.shape[0]
    flat_hot = (flat_routes[:, None] == expert_ids).astype(jnp.int32)
    slot_index = jnp.sum((jnp.cumsum(flat_hot, axis=0) - flat_hot) * flat_hot, axis=1)
    places = flat_routes * capacity + slot_index
    sources = (
        jnp.full((expert_count * capacity,), pair_count, jnp.int32)
        .at[places]
        .set(jnp.arange(pair_count, dtype=jnp.int32))
    )
    token_rows = jnp.where(sources < pair_count, sources // 2, tok_rows)
    routed_ext = jnp.concatenate([routed_low, jnp.zeros((1, model_width), jnp.bfloat16)], axis=0)
    outgoing = jnp.take(routed_ext, token_rows, axis=0).reshape(expert_count, capacity, model_width)
    grad_out = out_grad.astype(jnp.float32)
    grad_branch = (
        (gates[:, :, None] * grad_out[:, None, :])
        .astype(jnp.bfloat16)
        .reshape(pair_count, model_width)
    )
    branch_ext = jnp.concatenate([grad_branch, jnp.zeros((1, model_width), jnp.bfloat16)], axis=0)
    grad_outgoing = jnp.take(branch_ext, sources, axis=0).reshape(
        expert_count, capacity, model_width
    )
    up_list = expert_list(frozen_up, new_up)
    down_list = expert_list(frozen_down, new_down)
    results = []
    input_grads = []
    up_grads = []
    down_grads = []
    arrived = lax.all_to_all(outgoing, "wide", split_axis=0, concat_axis=1, tiled=True)
    for member in range(group_size):
        results.append(expert_forward(arrived[member], up_list[member], down_list[member]))
    returned = lax.all_to_all(jnp.stack(results), "wide", split_axis=1, concat_axis=0, tiled=True)
    grad_arrived = lax.all_to_all(grad_outgoing, "wide", split_axis=0, concat_axis=1, tiled=True)
    again_full = (
        lax.all_gather(new_in, "narrow", axis=1, tiled=True),
        lax.all_gather(new_out, "narrow", axis=1, tiled=True),
    )
    again_up = again_full[0]
    again_down = again_full[1]
    up_back = expert_list(frozen_up, again_up)
    down_back = expert_list(frozen_down, again_down)
    for member in range(group_size):
        active_low, row_grad, down_grad, up_grad = expert_backward(
            arrived[member],
            grad_arrived[member],
            up_back[member],
            down_back[member],
            member >= frozen_local,
        )
        input_grads.append(row_grad)
        if member >= frozen_local:
            down_grads.append(down_grad)
            up_grads.append(up_grad)
    sent_back = lax.all_to_all(
        jnp.stack(input_grads), "wide", split_axis=1, concat_axis=0, tiled=True
    )
    picked_rows = jnp.take(returned.reshape(expert_count * capacity, model_width), places, axis=0)
    picked_rows = picked_rows.astype(jnp.float32).reshape(tok_rows, 2, model_width)
    block_out = (after_attn + jnp.sum(gates[:, :, None] * picked_rows, axis=1)).astype(jnp.bfloat16)
    grad_gates = jnp.sum(grad_out[:, None, :] * picked_rows, axis=2)
    grad_rows = jnp.take(sent_back.reshape(expert_count * capacity, model_width), places, axis=0)
    grad_routed = jnp.sum(grad_rows.astype(jnp.float32).reshape(tok_rows, 2, model_width), axis=1)
    back_dense = (
        lax.all_gather(ln1_gain, ("wide", "narrow"), axis=0, tiled=True),
        lax.all_gather(w_qkv, ("wide", "narrow"), axis=0, tiled=True),
        lax.all_gather(w_out, ("wide", "narrow"), axis=0, tiled=True),
        lax.all_gather(ln2_gain, ("wide", "narrow"), axis=0, tiled=True),
        lax.all_gather(w_router, ("wide", "narrow"), axis=0, tiled=True),
    )
    weighted = jnp.sum(gates * grad_gates, axis=1, keepdims=True)
    grad_picked = gates * (grad_gates - weighted)
    grad_logits = jnp.sum(grad_picked[:, :, None] * route_hot, axis=1).astype(jnp.bfloat16)
    router_grad = lax.dot_general(
        routed_low, grad_logits, (((0,), (0,)), ((), ())), preferred_element_type=jnp.float32
    )
    grad_routed = grad_routed + lax.dot_general(
        grad_logits, back_dense[4], (((1,), (1,)), ((), ())), preferred_element_type=jnp.float32
    )
    gain_two_grad = jnp.sum(grad_routed * normed_two, axis=0)
    bias_two_grad = jnp.sum(grad_routed, axis=0)
    grad_after = grad_out + norm_back(
        grad_routed, normed_two, inv_two, back_dense[3].astype(jnp.float32)
    )
    grad_attn = grad_after.astype(jnp.bfloat16)
    out_proj_grad = lax.dot_general(
        mixed_low, grad_attn, (((0,), (0,)), ((), ())), preferred_element_type=jnp.float32
    )
    grad_mixed = lax.dot_general(
        grad_attn, back_dense[2], (((1,), (1,)), ((), ())), preferred_element_type=jnp.float32
    ).astype(jnp.bfloat16)
    grad_qkv = attend_backward(qkv_low, grad_mixed, log_totals)
    qkv_grad = lax.dot_general(
        normed_low, grad_qkv, (((0,), (0,)), ((), ())), preferred_element_type=jnp.float32
    )
    grad_normed = lax.dot_general(
        grad_qkv, back_dense[1], (((1,), (1,)), ((), ())), preferred_element_type=jnp.float32
    )
    gain_one_grad = jnp.sum(grad_normed * normed_one, axis=0)
    bias_one_grad = jnp.sum(grad_normed, axis=0)
    tokens_grad = grad_after + norm_back(
        grad_normed, normed_one, inv_one, back_dense[0].astype(jnp.float32)
    )
    expert_sums = (
        lax.psum_scatter(
            jnp.stack(up_grads).astype(jnp.bfloat16), "narrow", scatter_dimension=1, tiled=True
        ).astype(jnp.float32),
        lax.psum_scatter(
            jnp.stack(down_grads).astype(jnp.bfloat16), "narrow", scatter_dimension=1, tiled=True
        ).astype(jnp.float32),
    )
    dense_sums = (
        lax.psum_scatter(gain_one_grad, ("wide", "narrow"), scatter_dimension=0, tiled=True),
        lax.psum_scatter(bias_one_grad, ("wide", "narrow"), scatter_dimension=0, tiled=True),
        lax.psum_scatter(qkv_grad, ("wide", "narrow"), scatter_dimension=0, tiled=True),
        lax.psum_scatter(out_proj_grad, ("wide", "narrow"), scatter_dimension=0, tiled=True),
        lax.psum_scatter(gain_two_grad, ("wide", "narrow"), scatter_dimension=0, tiled=True),
        lax.psum_scatter(bias_two_grad, ("wide", "narrow"), scatter_dimension=0, tiled=True),
        lax.psum_scatter(router_grad, ("wide", "narrow"), scatter_dimension=0, tiled=True),
    )
    return (
        block_out,
        tokens_grad,
        dense_sums[0],
        dense_sums[1],
        dense_sums[2],
        dense_sums[3],
        dense_sums[4],
        dense_sums[5],
        dense_sums[6],
        expert_sums[0],
        expert_sums[1],
    )


def solution(mesh):
    placed = (
        P(("wide", "narrow"), None),
        P(("wide", "narrow"), None),
        P(("wide", "narrow"), None),
        P(("wide", "narrow")),
        P(("wide", "narrow")),
        P(("wide", "narrow")),
        P(("wide", "narrow"), None),
        P(("wide", "narrow"), None),
        P(("wide", "narrow")),
        P(("wide", "narrow")),
        P(("wide", "narrow"), None),
        P("wide", "narrow", None),
        P("wide", "narrow", None),
        P("wide", "narrow", None),
        P("wide", "narrow", None),
    )
    return jax.shard_map(
        local,
        mesh=mesh,
        in_specs=placed,
        out_specs=(
            P(("wide", "narrow"), None),
            P(("wide", "narrow"), None),
            P(("wide", "narrow")),
            P(("wide", "narrow")),
            P(("wide", "narrow"), None),
            P(("wide", "narrow"), None),
            P(("wide", "narrow")),
            P(("wide", "narrow")),
            P(("wide", "narrow"), None),
            P("wide", "narrow", None),
            P("wide", "narrow", None),
        ),
        check_vma=False,
    )
```

profile of v0, /device:TPU:0, one launch (start us, length us, event | category | flops | bytes accessed | tf_op | source)
XLA Modules:
  0.0 1291.3 jit_solution(691722688392959388)
XLA Ops:
  13.8 42.5 %all-reduce.12 = (bf16[768]{0:T(1024)(128)(2,1)S(1)}, bf16[768]{0:T(1024)(128)(2,1)S(1)}, bf16[768]{0:T(1024)(128)(2,1)S(1)}, bf16[768]{0:T(1024)(128)(2,1)S(1)}) all-reduce(bf16[768]{0:T(1024)(128)(2,1)S(1)} %dynamic-update-slice.1, bf16[768]{0:T(1024)(128)(2,1)S(1)} %dynamic-update-slice, ...), channel_id=1, replica_groups=mesh['wide'=8,'narrow'=4] {'wide','narrow'}, use_global_device_ids=true, to_apply=%add.3 | all-reduce | flops 3072 | bytes 12288
  81.6 127.5 %while.44 = (s32[]{:T(128)}, bf16[12,1024,64]{1,2,0:T(8,128)(2,1)}, f32[12,1024]{1,0:T(8,128)}, s32[12]{0:T(128)S(1)}, bf16[1024,2304]{1,0:T(8,128)(2,1)}, /*ind...) while((s32[]{:T(128)}, bf16[12,1024,64]{1,2,0:T(8,128)(2,1)}, ...), condition=%wide.region_5.6_spmd.clone, body=%wide.region_2.5_spmd.clone.sunk | while | flops 284228608 | bytes 30318920 | solution.py:74
  214.2 8.5 gather_fusion
  231.6 45.7 %all-to-all-done = bf16[16,160,768]{2,1,0:T(8,128)(2,1)} async-done(((bf16[16,160,768]{2,1,0:T(8,128)(2,1)}), bf16[16,160,768]{2,1,0:T(8,128)(2,1)}, u32[]{:S(2)}, u32[]{:S(2)}) %all-to-all-start) | async-done | bytes 3932192 | tf_op jit(solution)/shard_map/all_to_all | solution.py:258
  281.7 12.3 fusion.67
  293.9 14.5 %all-gather.12.cloned.1.call-done = bf16[1,768,3072]{2,1,0:T(8,128)(2,1)} async-done(((bf16[1,192,3072]{2,1,0:T(8,128)(2,1)}), bf16[1,768,3072]{2,1,0:T(8,128)(2,1)}) %all-gather.12.cloned.1.call-update) | async-done | bytes 4718608 | tf_op jit(solution)/shard_map/all_gather | solution.py:193
  308.5 12.2 fusion.73
  320.7 77.0 %all-gather.18.cloned.1.call-done = bf16[1,3072,768]{2,1,0:T(8,128)(2,1)} async-done(((bf16[1,768,768]{2,1,0:T(8,128)(2,1)}), bf16[1,3072,768]{2,1,0:T(8,128)(2,1)}) %all-gather.18.cloned.1.call-update) | async-done | bytes 4718608 | tf_op jit(solution)/shard_map/all_gather | solution.py:196
  397.7 14.8 %fusion.113 = bf16[1,1280,768]{2,1,0:T(8,128)(2,1)} fusion(bf16[1,3072,768]{2,1,0:T(8,128)(2,1)} %all-gather.18.cloned.1.call-done, f32[1280,3072]{1,0:T(8,128)} %fusion.67), kind=kOutput, calls=%fused_computation.136 | convolution fusion | flops 6076170240 | bytes 22413312 | tf_op jit(solution)/shard_map/dot_general | solution.py:140
  412.5 74.5 %all-gather.14.cloned.1.call-done = bf16[1,3072,768]{2,1,0:T(8,128)(2,1)} async-done(((bf16[1,768,768]{2,1,0:T(8,128)(2,1)}), bf16[1,3072,768]{2,1,0:T(8,128)(2,1)}) %all-gather.14.cloned.1.call-update) | async-done | bytes 4718608 | tf_op jit(solution)/shard_map/all_gather | solution.py:194
  487.0 14.4 %fusion.110 = bf16[1,1280,768]{2,1,0:T(8,128)(2,1)S(1)} fusion(bf16[1,3072,768]{2,1,0:T(8,128)(2,1)} %all-gather.14.cloned.1.call-done, f32[1280,3072]{1,0:T(8,128)} %fusion.73), kind=kOutput, calls=%fused_computation.135 | convolution fusion | flops 6076170240 | bytes 22413312 | tf_op jit(solution)/shard_map/dot_general | solution.py:140
  501.8 15.4 %copy.67 = bf16[2,1280,768]{2,0,1:T(2,128)(2,1)} copy(bf16[2,1280,768]{2,1,0:T(8,128)(2,1)S(1)} %pad_maximum_fusion) | data formatting | bytes 7864320 | tf_op jit(solution)/shard_map/stack | solution.py:261
  526.4 8.6 mul.352
  534.9 67.5 %all-gather = bf16[32,24,16]{1,2,0:T(8,128)(2,1)S(1)} all-gather(bf16[1,24,16]{1,2,0:T(8,128)(2,1)S(1)} %bitcast.187), channel_id=1, replica_groups=mesh['wide'=8,'narrow'=4] {'wide','narrow'}, dimensions={0}, use_global_device_ids=true | all-gather | bytes 25344 | tf_op jit(solution)/shard_map/all_gather | solution.py:190
  608.2 11.3 gather_fusion.2
  631.1 8.6 gather_fusion.1
  642.1 49.0 %all_to_all.60 = bf16[16,160,768]{2,1,0:T(8,128)(2,1)S(1)} all-to-all(bf16[16,160,768]{2,1,0:T(8,128)(2,1)S(1)} %broadcast_select_fusion), channel_id=1, replica_groups=mesh['wide'=8,'narrow'=4] {'wide'}, dimensions={0} | all-to-all | bytes 7864320 | tf_op jit(solution)/shard_map/all_to_all | solution.py:262
  692.1 16.5 %fusion.52 = bf16[1280,3072]{1,0:T(8,128)(2,1)S(1)} fusion(f32[1280,3072]{1,0:T(8,128)} %fusion.67, bf16[1280,768]{1,0:T(8,128)(2,1)S(1)} %bitcast.178, bf16[1,3072,768]{2,1,0:T(8,128)(2,1)S(1)} %bitcast.189), kind=kOutput, calls=%fused_computation.70 | convolution fusion | flops 6118440960 | bytes 30277632 | tf_op jit(solution)/shard_map/dot_general | solution.py:147
  719.7 15.0 %fusion.76 = bf16[1,3072,768]{2,1,0:T(8,128)(2,1)} fusion(bf16[1280,768]{1,0:T(8,128)(2,1)} %bitcast.179, f32[1280,3072]{1,0:T(8,128)} %fusion.67), kind=kOutput, calls=%fused_computation.103 | convolution fusion | flops 6077546496 | bytes 22413312 | tf_op jit(solution)/shard_map/dot_general | solution.py:154
  734.7 23.5 %fusion.105 = bf16[1,1280,768]{2,1,0:T(8,128)(2,1)} fusion(bf16[1,768,3072]{2,1,0:T(8,128)(2,1)} %all-gather.12.cloned.1.call-done, f32[1280,3072]{1,0:T(8,128)} %fusion.73, bf16[1280,768]{1,0:T(8,128)(2,1)S(1)} %bitcast.177, bf16[1,3072,768]{2,1,0:T(8,128)(2,1)} %all-gather.14.cloned.1.call-done), kind=kOutput, calls=%fused_computation.134 | convolution fusion | flops 12159221760 | bytes 29097984 | tf_op jit(solution)/shard_map/dot_general | solution.py:160
  758.3 10.4 fusion.116
  769.1 15.4 %copy.70 = bf16[2,1280,768]{2,0,1:T(2,128)(2,1)} copy(bf16[2,1280,768]{2,1,0:T(8,128)(2,1)S(1)} %pad_maximum_fusion.1) | data formatting | bytes 7864320 | tf_op jit(solution)/shard_map/stack | solution.py:284
  789.3 46.2 %all-to-all-done.3 = bf16[2,1280,768]{2,0,1:T(2,128)(2,1)} async-done(((bf16[2,1280,768]{2,0,1:T(2,128)(2,1)}), bf16[2,1280,768]{2,0,1:T(2,128)(2,1)}, u32[]{:S(2)}, u32[]{:S(2)}) %all-to-all-start.3) | async-done | bytes 3932192 | tf_op jit(solution)/shard_map/all_to_all | solution.py:283
  840.2 12.9 %gather_fusion.3 = bf16[2048,768]{1,0:T(8,128)(2,1)} fusion(bf16[2560,768]{1,0:T(8,128)(2,1)} %bitcast.170, s32[2048]{0:T(1024)S(1)} %broadcast_clamp_fusion), kind=kCustom, calls=%fused_computation.1.clone | custom fusion | bytes 6299648 | tf_op jit(solution)/shard_map/jit(_take)/gather | solution.py:290
  867.9 8.3 reshape.240
  876.2 12.2 reduce_sum.217
  892.6 29.8 %multiply_reduce_fusion.2 = f32[1024,768]{1,0:T(8,128)S(1)} fusion(f32[1024,2,768]{2,1,0:T(2,128)S(1)} %copy-done.6, f32[1024,2]{1,0:T(8,128)S(1)} %copy-done.15), kind=kLoop, calls=%fused_computation.83 | loop fusion | flops 2359296 | bytes 9445376 | tf_op jit(solution)/shard_map/reduce_sum | solution.py:288
  932.8 226.6 %while.45 = (s32[]{:T(128)}, bf16[12,3,1024,64]{2,3,0,1:T(8,128)(2,1)}, s32[12]{0:T(128)S(1)}, bf16[1024,2304]{1,0:T(8,128)(2,1)}, f32[12,1024]{1,0:T(8,128)}, /...) while((s32[]{:T(128)}, ...), condition=%wide.region_24.26_spmd.clone, body=%wide.region_22.25_spmd.clone.sunk | while | flops 683015168 | bytes 51270040 | solution.py:118
  1159.4 8.9 fusion.148
  1170.0 9.9 fusion.103
  1180.0 37.5 %all-reduce.11 = (f32[768]{0:T(1024)S(1)}, f32[768]{0:T(1024)S(1)}, f32[768]{0:T(1024)S(1)}, f32[768]{0:T(1024)S(1)}, f32[768,16]{0,1:T(8,128)S(1)}) all-reduce(f32[768]{0:T(1024)S(1)} %get-tuple-element.245, f32[768]{0:T(1024)S(1)} %get-tuple-element.250, ...), channel_id=2, replica_groups=mesh['wide'=8,'narrow'=4] {'wide','narrow'}, use_global_device_ids=true, to_apply=%region_28.30.clone | all-reduce | flops 15360 | bytes 122880
  1230.8 53.4 %reduce-scatter.6.cloned.1.call-done = f32[24,2304]{1,0:T(8,128)} async-done(((f32[768,2304]{1,0:T(8,128)}), f32[24,2304]{1,0:T(8,128)}) %reduce-scatter.6.cloned.1.call-update) | async-done | bytes 221200 | tf_op jit(solution)/shard_map/reduce_scatter | solution.py:343
  (453 shorter events, 459.3 us)
Async XLA Ops:
  7.2 49.0 %copy-start.9 = (bf16[1024,768]{1,0:T(8,128)(2,1)S(1)}, bf16[1024,768]{1,0:T(8,128)(2,1)}, u32[]{:S(2)}) copy-start(bf16[1024,768]{1,0:T(8,128)(2,1)} %param.21) | copy-start | bytes 4718596
  7.2 66.5 %all-gather.8.cloned.1.call-start = ((), (), s32[]{:S(2)}) async-start(), calls=%async_computation.8 | async-start | bytes 3649536 | tf_op jit(solution)/shard_map/all_gather | solution.py:186
  8.0 201.1 %all-gather.10.cloned.1.call-start = ((), (), s32[]{:S(2)}) async-start(), calls=%async_computation.9 | async-start | bytes 1216512 | tf_op jit(solution)/shard_map/all_gather | solution.py:187
  8.7 273.0 %all-gather.16.cloned.1.call-start = ((), (), s32[]{:S(2)}) async-start(), calls=%async_computation.12 | async-start | bytes 5898240 | tf_op jit(solution)/shard_map/all_gather | solution.py:195
  9.4 299.0 %all-gather.12.cloned.1.call-start = ((), (), s32[]{:S(2)}) async-start(), calls=%async_computation.10 | async-start | bytes 5898240 | tf_op jit(solution)/shard_map/all_gather | solution.py:193
  10.0 387.7 %all-gather.18.cloned.1.call-start = ((), (), s32[]{:S(2)}) async-start(), calls=%async_computation.13 | async-start | bytes 5898240 | tf_op jit(solution)/shard_map/all_gather | solution.py:196
  56.2 25.4 %copy-start.39 = (f32[768]{0:T(1024)}, f32[768]{0:T(1024)S(1)}, u32[]{:S(2)}) copy-start(f32[768]{0:T(1024)S(1)} %convert_element_type.140) | copy-start | bytes 9220
  56.2 25.4 %copy-start.34 = (f32[768]{0:T(1024)}, f32[768]{0:T(1024)S(1)}, u32[]{:S(2)}) copy-start(f32[768]{0:T(1024)S(1)} %convert_element_type.139) | copy-start | bytes 9220
  56.5 25.1 %copy-start.30 = (f32[1024]{0:T(1024)}, f32[1024]{0:T(1024)S(1)}, u32[]{:S(2)}) copy-start(f32[1024]{0:T(1024)S(1)} %broadcast_multiply_fusion.6) | copy-start | bytes 12292
  57.2 24.4 %copy-start.36 = (f32[1024]{0:T(1024)}, f32[1024]{0:T(1024)S(1)}, u32[]{:S(2)}) copy-start(f32[1024]{0:T(1024)S(1)} %add_rsqrt_fusion.1) | copy-start | bytes 12292
  57.2 155.8 %copy-start.26 = (f32[768]{0:T(1024)}, f32[768]{0:T(1024)S(1)}, u32[]{:S(2)}) copy-start(f32[768]{0:T(1024)S(1)} %convert_element_type.143) | copy-start | bytes 9220
  214.1 388.8 %copy-start.7 = (bf16[1024,768]{1,0:T(8,128)(2,1)}, bf16[1024,768]{1,0:T(8,128)(2,1)S(1)}, u32[]{:S(2)}) copy-start(bf16[1024,768]{1,0:T(8,128)(2,1)S(1)} %add_convert_fusion.1) | copy-start | bytes 4718596
  226.5 50.9 %all-to-all-start = ((bf16[16,160,768]{2,1,0:T(8,128)(2,1)}), bf16[16,160,768]{2,1,0:T(8,128)(2,1)}, u32[]{:S(2)}, u32[]{:S(2)}) async-start(bf16[16,160,768]{2,1,0:T(8,128)(2,1)} %broadcast_select_fusion.1), calls=%async_computation | async-start | bytes 7864320 | tf_op jit(solution)/shard_map/all_to_all | solution.py:258
  231.0 255.9 %all-gather.14.cloned.1.call-start = ((), (), s32[]{:S(2)}) async-start(), calls=%async_computation.11 | async-start | bytes 5898240 | tf_op jit(solution)/shard_map/all_gather | solution.py:194
  517.2 86.3 %all-to-all-start.1 = ((bf16[2,1280,768]{2,0,1:T(2,128)(2,1)}), bf16[2,1280,768]{2,0,1:T(2,128)(2,1)}, u32[]{:S(2)}, u32[]{:S(2)}) async-start(bf16[2,1280,768]{2,0,1:T(2,128)(2,1)} %copy.67), calls=%async_computation.1 | async-start | bytes 7864320 | tf_op jit(solution)/shard_map/all_to_all | solution.py:261
  521.9 703.1 %reduce-scatter.10.cloned.1.call-start = ((), (), s32[]{:S(2)}) async-start(), calls=%async_computation.16 | async-start | bytes 5898240 | tf_op jit(solution)/shard_map/reduce_scatter | solution.py:333
  526.4 76.4 %copy-start.41 = (s32[1024]{0:T(1024)S(1)}, s32[1024]{0:T(1024)}, u32[]{:S(2)}) copy-start(s32[1024]{0:T(1024)} %param.24) | copy-start | bytes 12292
  526.4 77.0 %copy-start.22 = (s32[1024,2]{0,1:T(2,128)S(1)}, s32[1024,2]{0,1:T(2,128)}, u32[]{:S(2)}) copy-start(s32[1024,2]{0,1:T(2,128)} %param.23) | copy-start | bytes 24580
  602.9 16.6 %copy-start.32 = (pred[2048]{0:T(1024)(128)(4,1)}, pred[2048]{0:T(1024)(128)(4,1)S(1)}, u32[]{:S(2)}) copy-start(pred[2048]{0:T(1024)(128)(4,1)S(1)} %compare_and_fusion.2) | copy-start | bytes 6148
  642.1 49.3 %slice-start = ((s8[4718592]{0:T(1024)(128)(4,1)}), s8[4194304]{0:T(1024)(128)(4,1)S(1)}, s32[]{:S(2)}) async-start(s8[4718592]{0:T(1024)(128)(4,1)} %bitcast.188), calls=%async_computation.18 | async-start | bytes 8388608
  691.4 17.2 %copy-start.17 = (bf16[1,8,160,768]{3,2,0,1:T(8,128)(2,1)}, bf16[1,8,160,768]{3,2,0,1:T(8,128)(2,1)S(1)}, u32[]{:S(2)}) copy-start(bf16[1,8,160,768]{3,2,0,1:T(8,128)(2,1)S(1)} %get-tuple-element.293) | copy-start | bytes 5898244
  692.1 19.6 %copy-start.16 = (bf16[1,8,160,768]{3,2,0,1:T(8,128)(2,1)S(1)}, bf16[1,8,160,768]{3,2,0,1:T(8,128)(2,1)}, u32[]{:S(2)}) copy-start(bf16[1,8,160,768]{3,2,0,1:T(8,128)(2,1)} %get-tuple-element.295) | copy-start | bytes 5898244
  719.7 508.3 %reduce-scatter.12.cloned.1.call-start = ((), (), s32[]{:S(2)}) async-start(), calls=%async_computation.17 | async-start | bytes 5898240 | tf_op jit(solution)/shard_map/reduce_scatter | solution.py:336
  784.5 51.0 %all-to-all-start.3 = ((bf16[2,1280,768]{2,0,1:T(2,128)(2,1)}), bf16[2,1280,768]{2,0,1:T(2,128)(2,1)}, u32[]{:S(2)}, u32[]{:S(2)}) async-start(bf16[2,1280,768]{2,0,1:T(2,128)(2,1)} %copy.70), calls=%async_computation.3 | async-start | bytes 7864320 | tf_op jit(solution)/shard_map/all_to_all | solution.py:283
  789.1 441.7 %reduce-scatter.8.cloned.1.call-start = ((), (), s32[]{:S(2)}) async-start(), calls=%async_computation.15 | async-start | bytes 2433024 | tf_op jit(solution)/shard_map/reduce_scatter | solution.py:344
  892.6 29.8 %copy-start.13 = (bf16[1024,768]{1,0:T(8,128)(2,1)S(1)}, bf16[1024,768]{1,0:T(8,128)(2,1)}, u32[]{:S(2)}) copy-start(bf16[1024,768]{1,0:T(8,128)(2,1)} %param.22) | copy-start | bytes 4718596
  929.3 355.0 %reduce-scatter.6.cloned.1.call-start = ((), (), s32[]{:S(2)}) async-start(), calls=%async_computation.14 | async-start | bytes 7299072 | tf_op jit(solution)/shard_map/reduce_scatter | solution.py:343
  932.7 226.6 %copy-start.10 = (bf16[1024,768]{1,0:T(8,128)(2,1)S(1)}, bf16[1024,768]{1,0:T(8,128)(2,1)}, u32[]{:S(2)}) copy-start(bf16[1024,768]{1,0:T(8,128)(2,1)} %param.21) | copy-start | bytes 4718596
  932.7 226.6 %copy-start.31 = (f32[1024]{0:T(1024)S(1)}, f32[1024]{0:T(1024)}, u32[]{:S(2)}) copy-start(f32[1024]{0:T(1024)} %copy-done.30) | copy-start | bytes 12292
  932.8 226.6 %copy-start.35 = (f32[768]{0:T(1024)S(1)}, f32[768]{0:T(1024)}, u32[]{:S(2)}) copy-start(f32[768]{0:T(1024)} %copy-done.34) | copy-start | bytes 9220
  932.8 226.6 %copy-start.37 = (f32[1024]{0:T(1024)S(1)}, f32[1024]{0:T(1024)}, u32[]{:S(2)}) copy-start(f32[1024]{0:T(1024)} %copy-done.36) | copy-start | bytes 12292
  932.8 226.6 %copy-start.40 = (f32[768]{0:T(1024)S(1)}, f32[768]{0:T(1024)}, u32[]{:S(2)}) copy-start(f32[768]{0:T(1024)} %copy-done.39) | copy-start | bytes 9220
  (54 other events, 241.4 us)
Sparse Core Ops, SparseCore 0:
  10.8 62.8 all-gather.7
  76.5 52.7 all-gather.9
  130.9 88.3 all-gather.15
  220.7 87.7 all-gather.11
  309.9 87.7 all-gather.17
  399.2 87.7 all-gather.13
  719.8 81.5 reduce-scatter.9
  803.8 85.7 reduce-scatter.11
  929.4 95.8 reduce-scatter.7
  1168.5 115.7 reduce-scatter.5
where the time goes:
time: 1300 us; the launch traced here: 1290 us
  matrix products  374 us (29%)
  waiting for transfers between devices  317 us (24%)
  local copies, waits for them, and re-layouts  221 us (17%)
  blocking collectives  196 us (15%)
  other arithmetic  113 us (9%)
  loops' own time  40 us (3%)
  between operations  15.3 us (1%)
  starting transfers between devices  14.5 us (1%)
    unnamed x2, blocking collectives  80 us
    all_gather x1, waiting for transfers between devices, local(): lax.all_gather(new_out, 'narrow', axis=1, tiled=True)  77 us
    all_gather x1, waiting for transfers between devices, local(): lax.all_gather(frozen_out, 'narrow', axis=1, tiled=True)  74.5 us
    all_gather x1, blocking collectives, local(): lax.all_gather(w_router, ('wide', 'narrow'), axis=0, tiled=True)  67.5 us
    dot_general x24, matrix products, head_scores(): lax.dot_general(queries, key_rows, (((1,), (1,)), ((), ())), preferred_el...  65.4 us
    reduce_scatter x1, waiting for transfers between devices, local(): lax.psum_scatter(qkv_grad, ('wide', 'narrow'), scatter_dimension=0, tiled...  53.4 us
    all_to_all x1, blocking collectives, local(): lax.all_to_all(grad_outgoing, 'wide', split_axis=0, concat_axis=1, tiled=...  49 us
    all_to_all x1, waiting for transfers between devices, local(): lax.all_to_all(jnp.stack(input_grads), 'wide', split_axis=1, concat_axis=...  46.2 us
  transfers between devices with their start and end apart: 13, of which 7 were waited for; matrix products, arithmetic and copies ran while one was open for 44% of the time, Pallas kernels for 0%

commit v1 on v0

--- a/solution.py
+++ b/solution.py
@@ -1,11 +1,14 @@
 import jax
 import jax.numpy as jnp
 from jax import lax
+from jax.experimental import pallas as pl
+from jax.experimental.pallas import tpu as pltpu
 from jax.sharding import PartitionSpec as P
 
 HEADS = 12
 HD = 64
 SEQ = 1024
+BLK = 256
 
 
 EPSILON = 1e-05
@@ -33,101 +36,87 @@
     )
 
 
-def causal(length):
-    places = jnp.arange(length, dtype=jnp.int32)
-    return places[:, None] >= places[None, :]
-
-
-def head_columns(seq_block, head_idx):
-    model_width = HEADS * HD
-    queries = lax.dynamic_slice_in_dim(seq_block, head_idx * HD, HD, 1)
-    key_rows = lax.dynamic_slice_in_dim(seq_block, model_width + head_idx * HD, HD, 1)
-    value_rows = lax.dynamic_slice_in_dim(seq_block, 2 * model_width + head_idx * HD, HD, 1)
-    return (queries, key_rows, value_rows)
-
-
-def head_scores(queries, key_rows, allowed):
-    scores = lax.dot_general(
-        queries, key_rows, (((1,), (1,)), ((), ())), preferred_element_type=jnp.float32
-    ) * HD ** (-0.5)
-    return jnp.where(allowed, scores, NEGATIVE)
-
-
-def attend_forward(qkv_low):
-    model_width = HEADS * HD
-    allowed = causal(SEQ)
-
-    def per_sequence(seq_block):
-
-        def per_head(head_idx):
-            queries, key_rows, value_rows = head_columns(seq_block, head_idx)
-            scores = head_scores(queries, key_rows, allowed)
-            row_top = jnp.max(scores, axis=1, keepdims=True)
-            exponent = jnp.exp(scores - row_top)
-            row_total = jnp.sum(exponent, axis=1, keepdims=True)
-            probs_low = (exponent / row_total).astype(jnp.bfloat16)
-            mixed = jnp.dot(probs_low, value_rows, preferred_element_type=jnp.float32).astype(
-                jnp.bfloat16
-            )
-            return (mixed, (row_top + jnp.log(row_total))[:, 0])
-
-        mixed, log_total = lax.map(per_head, jnp.arange(HEADS, dtype=jnp.int32))
-        return (jnp.transpose(mixed, (1, 0, 2)).reshape(SEQ, model_width), log_total)
-
-    return lax.map(per_sequence, qkv_low.reshape(-1, SEQ, 3 * model_width))
-
-
-def attend_backward(qkv_low, grad_mixed, log_totals):
-    model_width = HEADS * HD
-    allowed = causal(SEQ)
-    score_scale = HD ** (-0.5)
-
-    def per_sequence(operands):
-        seq_block, grad_block, log_seq = operands
-
-        def per_head(head_idx):
-            queries, key_rows, value_rows = head_columns(seq_block, head_idx)
-            grad_head = lax.dynamic_slice_in_dim(grad_block, head_idx * HD, HD, 1)
-            log_head = lax.dynamic_index_in_dim(log_seq, head_idx, 0, keepdims=False)
-            scores = head_scores(queries, key_rows, allowed)
-            probs = jnp.exp(scores - log_head[:, None])
-            probs_low = probs.astype(jnp.bfloat16)
-            grad_probs = lax.dot_general(
-                grad_head, value_rows, (((1,), (1,)), ((), ())), preferred_element_type=jnp.float32
-            )
-            grad_values = lax.dot_general(
-                probs_low, grad_head, (((0,), (0,)), ((), ())), preferred_element_type=jnp.float32
-            )
-            grad_scores = (
-                probs * (grad_probs - jnp.sum(probs * grad_probs, axis=1, keepdims=True))
-            ).astype(jnp.bfloat16)
-            grad_queries = (
-                jnp.dot(grad_scores, key_rows, preferred_element_type=jnp.float32) * score_scale
-            )
-            grad_keys = (
-                lax.dot_general(
-                    grad_scores,
-                    queries,
-                    (((0,), (0,)), ((), ())),
-                    preferred_element_type=jnp.float32,
-                )
-                * score_scale
-            )
-            return jnp.stack([grad_queries, grad_keys, grad_values])
-
-        head_grads = lax.map(per_head, jnp.arange(HEADS, dtype=jnp.int32))
-        return (
-            jnp.transpose(head_grads, (2, 1, 0, 3))
-            .reshape(SEQ, 3 * model_width)
-            .astype(jnp.bfloat16)
-        )
-
-    operands = (
-        qkv_low.reshape(-1, SEQ, 3 * model_width),
-        grad_mixed.reshape(-1, SEQ, model_width),
-        log_totals,
-    )
-    return lax.map(per_sequence, operands).reshape(-1, 3 * model_width)
+def _nt(a,b): return lax.dot_general(a,b,(((1,),(1,)),((),())),preferred_element_type=jnp.float32)
+def _tn(a,b): return lax.dot_general(a,b,(((0,),(0,)),((),())),preferred_element_type=jnp.float32)
+
+def attn_fwd_kernel(q_ref,k_ref,v_ref,o_ref,lse_ref):
+    hp=pl.program_id(0); S=q_ref.shape[0]
+    @pl.when(hp==0)
+    def _(): lse_ref[...]=jnp.zeros_like(lse_ref)
+    lane=lax.broadcasted_iota(jnp.int32,(BLK,128),1)
+    row=lax.broadcasted_iota(jnp.int32,(BLK,BLK),0); col=lax.broadcasted_iota(jnp.int32,(BLK,BLK),1)
+    for i in range(S//BLK):
+        sl=pl.ds(i*BLK,BLK)
+        q=q_ref[sl,:]*jnp.bfloat16(HD**-0.5)
+        kw=(i+1)*BLK
+        kb=k_ref[0:kw,:]; vb=v_ref[0:kw,:]
+        outs=[]; tops=[]
+        for h in range(2):
+            mine=(lane<HD) if h==0 else (lane>=HD)
+            s=_nt(jnp.where(mine,q,jnp.bfloat16(0)),kb)
+            diag=jnp.where(row>=col,s[:,kw-BLK:],NEGATIVE)
+            s=diag if i==0 else jnp.concatenate([s[:,:kw-BLK],diag],axis=1)
+            m=jnp.max(s,axis=1,keepdims=True)
+            e=jnp.exp(s-m)
+            l=jnp.sum(e,axis=1,keepdims=True)
+            outs.append(jnp.dot(e.astype(jnp.bfloat16),vb,preferred_element_type=jnp.float32)/l)
+            tops.append(m+jnp.log(l))
+        o_ref[sl,:]=jnp.where(lane<HD,outs[0],outs[1]).astype(jnp.bfloat16)
+        lse_ref[sl,:]=jnp.where(lane==2*hp,tops[0],jnp.where(lane==2*hp+1,tops[1],lse_ref[sl,:]))
+
+def attn_fwd(qkv):
+    S=qkv.shape[0]; D=HEADS*HD; n=D//128
+    return pl.pallas_call(attn_fwd_kernel,grid=(n,),
+        in_specs=[pl.BlockSpec((S,128),lambda h:(0,h)),pl.BlockSpec((S,128),lambda h:(0,n+h)),pl.BlockSpec((S,128),lambda h:(0,2*n+h))],
+        out_specs=[pl.BlockSpec((S,128),lambda h:(0,h)),pl.BlockSpec((S,128),lambda h:(0,0))],
+        out_shape=[jax.ShapeDtypeStruct((S,D),jnp.bfloat16),jax.ShapeDtypeStruct((S,128),jnp.float32)],
+        name="attn_fwd")(qkv,qkv,qkv)
+
+def attn_bwd_kernel(q_ref,k_ref,v_ref,g_ref,o_ref,lse_ref,out_ref,dq_ref):
+    hp=pl.program_id(0); S=q_ref.shape[0]
+    lane=lax.broadcasted_iota(jnp.int32,(BLK,128),1)
+    krow=lax.broadcasted_iota(jnp.int32,(BLK,BLK),0); qcol=lax.broadcasted_iota(jnp.int32,(BLK,BLK),1)
+    q=q_ref[...]*jnp.bfloat16(HD**-0.5)
+    g=g_ref[...]
+    prod=g.astype(jnp.float32)*o_ref[...].astype(jnp.float32)
+    hi=prod.astype(jnp.bfloat16); lo=(prod-hi.astype(jnp.float32)).astype(jnp.bfloat16)
+    l8=lax.broadcasted_iota(jnp.int32,(16,128),1); r8=lax.broadcasted_iota(jnp.int32,(16,128),0)
+    pick=jnp.where((l8//HD)==r8,1.0,0.0).astype(jnp.bfloat16)
+    delta=_nt(pick,hi)+_nt(pick,lo)
+    dq_ref[...]=jnp.zeros_like(dq_ref)
+    for j in range(S//BLK):
+        sl=pl.ds(j*BLK,BLK); q0=j*BLK
+        kb=k_ref[sl,:]; vb=v_ref[sl,:]
+        qs=q[q0:,:]; gs=g[q0:,:]
+        dvs=[];dks=[]
+        acc=None
+        for h in range(2):
+            mine=(lane<HD) if h==0 else (lane>=HD)
+            km=jnp.where(mine,kb,jnp.bfloat16(0)); vm=jnp.where(mine,vb,jnp.bfloat16(0))
+            st=_nt(km,qs)-lse_ref[pl.ds(2*hp+h,1),q0:]
+            diag=jnp.where(qcol>=krow,st[:,:BLK],NEGATIVE)
+            st=diag if q0+BLK==S else jnp.concatenate([diag,st[:,BLK:]],axis=1)
+            pt=jnp.exp(st)
+            dpt=_nt(vm,gs)
+            ds=(pt*(dpt-delta[h:h+1,q0:])).astype(jnp.bfloat16)
+            dvs.append(jnp.dot(pt.astype(jnp.bfloat16),gs,preferred_element_type=jnp.float32))
+            dks.append(jnp.dot(ds,qs,preferred_element_type=jnp.float32))
+            t=_tn(ds,km)
+            acc=t if acc is None else acc+t
+        dq_ref[pl.ds(q0,S-q0),:]+=acc
+        out_ref[1,sl,:]=jnp.where(lane<HD,dks[0],dks[1]).astype(jnp.bfloat16)
+        out_ref[2,sl,:]=jnp.where(lane<HD,dvs[0],dvs[1]).astype(jnp.bfloat16)
+    out_ref[0]=(dq_ref[...]*HD**-0.5).astype(jnp.bfloat16)
+
+def attn_bwd(qkv,g,o,lse_rows):
+    S=qkv.shape[0]; D=HEADS*HD; n=D//128
+    return pl.pallas_call(attn_bwd_kernel,grid=(n,),
+        in_specs=[pl.BlockSpec((S,128),lambda h:(0,h)),pl.BlockSpec((S,128),lambda h:(0,n+h)),pl.BlockSpec((S,128),lambda h:(0,2*n+h)),
+                  pl.BlockSpec((S,128),lambda h:(0,h)),pl.BlockSpec((S,128),lambda h:(0,h)),pl.BlockSpec(lse_rows.shape,lambda h:(0,0))],
+        out_specs=pl.BlockSpec((3,S,128),lambda h:(0,0,h)),
+        out_shape=jax.ShapeDtypeStruct((3,S,D),jnp.bfloat16),
+        scratch_shapes=[pltpu.VMEM((S,128),jnp.float32)],
+        name="attn_bwd")(qkv,qkv,qkv,g,o,lse_rows)
 
 
 def expert_list(frozen_part, new_part):
@@ -210,8 +199,8 @@
     qkv_low = jnp.dot(normed_low, dense_full[2], preferred_element_type=jnp.float32).astype(
         jnp.bfloat16
     )
-    mixed_low, log_totals = attend_forward(qkv_low)
-    mixed_low = mixed_low.reshape(tok_rows, model_width)
+    mixed_low, log_totals = attn_fwd(qkv_low)
+    log_rows = jnp.transpose(log_totals)[:16]
     after_attn = inputs_full + jnp.dot(mixed_low, dense_full[3], preferred_element_type=jnp.float32)
     hidden_two, normed_two, inv_two = layer_norm(
         after_attn, dense_full[4].astype(jnp.float32), dense_full[5].astype(jnp.float32)
@@ -260,12 +249,8 @@
         results.append(expert_forward(arrived[member], up_list[member], down_list[member]))
     returned = lax.all_to_all(jnp.stack(results), "wide", split_axis=1, concat_axis=0, tiled=True)
     grad_arrived = lax.all_to_all(grad_outgoing, "wide", split_axis=0, concat_axis=1, tiled=True)
-    again_full = (
-        lax.all_gather(new_in, "narrow", axis=1, tiled=True),
-        lax.all_gather(new_out, "narrow", axis=1, tiled=True),
-    )
-    again_up = again_full[0]
-    again_down = again_full[1]
+    again_up = new_up
+    again_down = new_down
     up_back = expert_list(frozen_up, again_up)
     down_back = expert_list(frozen_down, again_down)
     for member in range(group_size):
@@ -289,13 +274,7 @@
     grad_gates = jnp.sum(grad_out[:, None, :] * picked_rows, axis=2)
     grad_rows = jnp.take(sent_back.reshape(expert_count * capacity, model_width), places, axis=0)
     grad_routed = jnp.sum(grad_rows.astype(jnp.float32).reshape(tok_rows, 2, model_width), axis=1)
-    back_dense = (
-        lax.all_gather(ln1_gain, ("wide", "narrow"), axis=0, tiled=True),
-        lax.all_gather(w_qkv, ("wide", "narrow"), axis=0, tiled=True),
-        lax.all_gather(w_out, ("wide", "narrow"), axis=0, tiled=True),
-        lax.all_gather(ln2_gain, ("wide", "narrow"), axis=0, tiled=True),
-        lax.all_gather(w_router, ("wide", "narrow"), axis=0, tiled=True),
-    )
+    back_dense = (dense_full[0], dense_full[2], dense_full[3], dense_full[4], dense_full[6])
     weighted = jnp.sum(gates * grad_gates, axis=1, keepdims=True)
     grad_picked = gates * (grad_gates - weighted)
     grad_logits = jnp.sum(grad_picked[:, :, None] * route_hot, axis=1).astype(jnp.bfloat16)
@@ -317,7 +296,8 @@
     grad_mixed = lax.dot_general(
         grad_attn, back_dense[2], (((1,), (1,)), ((), ())), preferred_element_type=jnp.float32
     ).astype(jnp.bfloat16)
-    grad_qkv = attend_backward(qkv_low, grad_mixed, log_totals)
+    parts = attn_bwd(qkv_low, grad_mixed, mixed_low, log_rows)
+    grad_qkv = jnp.concatenate([parts[0], parts[1], parts[2]], axis=1)
     qkv_grad = lax.dot_general(
         normed_low, grad_qkv, (((0,), (0,)), ((), ())), preferred_element_type=jnp.float32
     )

time: 1300 us -> 1170 us (0.900)
  matrix products: 374 us -> 166 us
  waiting for transfers between devices: 317 us -> 483 us
  local copies, waits for them, and re-layouts: 221 us -> 154 us
  Pallas kernels: 0 us -> 48.6 us
  loops' own time: 40 us -> 0 us
  other arithmetic: 113 us -> 82.9 us
    dot_general x84 -> x0, matrix products: 205 us -> none  [the longest x24 65.4 us: head_scores(): lax.dot_general(queries, key_rows, (((1,), (1,)), ((), ())), preferred_el...]
    all_gather x1, waiting for transfers between devices: 0.01 us -> 77 us  [local(): lax.all_gather(new_in, 'narrow', axis=1, tiled=True)]
    reduce_scatter x1, waiting for transfers between devices: 53.4 us -> 113 us  [local(): lax.psum_scatter(qkv_grad, ('wide', 'narrow'), scatter_dimension=0, tiled...]
    pallas_call x0 -> x2, Pallas kernels: none -> 48.6 us  [the longest x1 26.5 us: attn_bwd(): pl.pallas_call(attn_bwd_kernel, grid=(n,), in_specs=[pl.BlockSpec((S, 128...]
    another operation x2 -> x0, loops' own time: 40 us -> none  [the longest x1 31.9 us: per_sequence(): head_grads = lax.map(per_head, jnp.arange(HEADS, dtype=jnp.int32))]
    while x48 -> x0, local copies, waits for them, and re-layouts: 39.4 us -> none
    all_gather x1, waiting for transfers between devices: 0.01 us -> 25.9 us  [local(): lax.all_gather(w_out, ('wide', 'narrow'), axis=0, tiled=True)]
    dynamic_slice x36 -> x0, local copies, waits for them, and re-layouts: 23.2 us -> none  [the longest x24 14 us: per_sequence(): mixed, log_total = lax.map(per_head, jnp.arange(HEADS, dtype=jnp.int32))]
  transfers between devices with their start and end apart: 13 -> 13, of which waited for: 7 -> 9; matrix products, arithmetic and copies ran while one was open for 44% -> 26% of each run, Pallas kernels for 0% -> 4%
where the time goes in v1:
time: 1170 us; the launch traced here: 1160 us
  waiting for transfers between devices  483 us (41%)
  blocking collectives  197 us (17%)
  matrix products  166 us (14%)
  local copies, waits for them, and re-layouts  154 us (13%)
  other arithmetic  82.9 us (7%)
  Pallas kernels  48.6 us (4%)
  between operations  15.5 us (1%)
  starting transfers between devices  14.4 us (1%)
    reduce_scatter x1, waiting for transfers between devices, local(): lax.psum_scatter(qkv_grad, ('wide', 'narrow'), scatter_dimension=0, tiled...  113 us
    unnamed x2, blocking collectives  80.3 us
    all_gather x1, waiting for transfers between devices, local(): lax.all_gather(new_in, 'narrow', axis=1, tiled=True)  77 us
    all_gather x1, waiting for transfers between devices, local(): lax.all_gather(frozen_out, 'narrow', axis=1, tiled=True)  77 us
    all_gather x1, waiting for transfers between devices, local(): lax.all_gather(new_out, 'narrow', axis=1, tiled=True)  74.5 us
    all_gather x1, blocking collectives, local(): lax.all_gather(w_router, ('wide', 'narrow'), axis=0, tiled=True)  68.1 us
    all_to_all x1, blocking collectives, local(): lax.all_to_all(grad_outgoing, 'wide', split_axis=0, concat_axis=1, tiled=...  48.7 us
    all_to_all x1, waiting for transfers between devices, local(): lax.all_to_all(jnp.stack(input_grads), 'wide', split_axis=1, concat_axis=...  46.2 us
  transfers between devices with their start and end apart: 13, of which 9 were waited for; matrix products, arithmetic and copies ran while one was open for 26% of the time, Pallas kernels for 4%

profile of v1, /device:TPU:0, one launch (start us, length us, event | category | flops | bytes accessed | tf_op | source)
XLA Modules:
  0.0 1161.9 jit_solution(14848031769934607050)
XLA Ops:
  18.3 42.2 %all-reduce.12 = (bf16[768]{0:T(1024)(128)(2,1)S(1)}, bf16[768]{0:T(1024)(128)(2,1)S(1)}, bf16[768]{0:T(1024)(128)(2,1)S(1)}, bf16[768]{0:T(1024)(128)(2,1)S(1)}) all-reduce(bf16[768]{0:T(1024)(128)(2,1)S(1)} %dynamic-update-slice.1, bf16[768]{0:T(1024)(128)(2,1)S(1)} %dynamic-update-slice, ...), channel_id=1, replica_groups=mesh['wide'=8,'narrow'=4] {'wide','narrow'}, use_global_device_ids=true, to_apply=%add.3 | all-reduce | flops 3072 | bytes 12288
  81.4 22.1 %attn_fwd.1 = (bf16[1024,768]{1,0:T(8,128)(2,1)}, f32[1024,128]{1,0:T(8,128)}) custom-call(bf16[1024,2304]{1,0:T(8,128)(2,1)} %convolution_convert_fusion.q_ref.k_ref.v_ref, bf16[1024,2304]{1,0:T(8,128)(2,1)} %convolution_convert_fusion.q_ref.k_ref.v_ref, bf16[1024,2304]{1,0:T(8,128)(2,1)} %convolution_convert_fusion.q_ref.k_ref.v_ref), custom_call_target="tpu_custom_call" | custom-call | tf_op jit(solution)/shard_map/attn_fwd/pallas_call | solution.py:69
  103.5 25.9 %all-gather.10.cloned.1.call-done = bf16[768,768]{1,0:T(8,128)(2,1)} async-done(((bf16[24,768]{1,0:T(8,128)(2,1)}), bf16[768,768]{1,0:T(8,128)(2,1)}) %all-gather.10.cloned.1.call-update) | async-done | bytes 1179664 | tf_op jit(solution)/shard_map/all_gather | solution.py:176
  134.9 8.6 gather_fusion
  152.3 45.7 %all-to-all-done = bf16[16,160,768]{2,1,0:T(8,128)(2,1)} async-done(((bf16[16,160,768]{2,1,0:T(8,128)(2,1)}), bf16[16,160,768]{2,1,0:T(8,128)(2,1)}, u32[]{:S(2)}, u32[]{:S(2)}) %all-to-all-start) | async-done | bytes 3932192 | tf_op jit(solution)/shard_map/all_to_all | solution.py:247
  202.3 16.9 %all-gather.12.cloned.1.call-done = bf16[1,768,3072]{2,1,0:T(8,128)(2,1)} async-done(((bf16[1,192,3072]{2,1,0:T(8,128)(2,1)}), bf16[1,768,3072]{2,1,0:T(8,128)(2,1)}) %all-gather.12.cloned.1.call-update) | async-done | bytes 4718608 | tf_op jit(solution)/shard_map/all_gather | solution.py:182
  219.3 12.3 %fusion.34 = f32[1280,3072]{1,0:T(8,128)} fusion(bf16[1280,768]{1,0:T(8,128)(2,1)} %bitcast.136, bf16[1,768,3072]{2,1,0:T(8,128)(2,1)} %all-gather.12.cloned.1.call-done), kind=kOutput, calls=%fused_computation.53 | convolution fusion | flops 6039797760 | bytes 22413312 | tf_op jit(solution)/shard_map/dot_general | solution.py:127
  231.5 77.0 %all-gather.16.cloned.1.call-done = bf16[1,768,3072]{2,1,0:T(8,128)(2,1)} async-done(((bf16[1,192,3072]{2,1,0:T(8,128)(2,1)}), bf16[1,768,3072]{2,1,0:T(8,128)(2,1)}) %all-gather.16.cloned.1.call-update) | async-done | bytes 4718608 | tf_op jit(solution)/shard_map/all_gather | solution.py:184
  308.5 12.3 %fusion.28 = f32[1280,3072]{1,0:T(8,128)} fusion(bf16[1280,768]{1,0:T(8,128)(2,1)} %bitcast.131, bf16[1,768,3072]{2,1,0:T(8,128)(2,1)} %all-gather.16.cloned.1.call-done), kind=kOutput, calls=%fused_computation.48 | convolution fusion | flops 6039797760 | bytes 22413312 | tf_op jit(solution)/shard_map/dot_general | solution.py:127
  320.8 77.0 %all-gather.14.cloned.1.call-done = bf16[1,3072,768]{2,1,0:T(8,128)(2,1)} async-done(((bf16[1,768,768]{2,1,0:T(8,128)(2,1)}), bf16[1,3072,768]{2,1,0:T(8,128)(2,1)}) %all-gather.14.cloned.1.call-update) | async-done | bytes 4718608 | tf_op jit(solution)/shard_map/all_gather | solution.py:183
  397.8 14.8 %fusion.71 = bf16[1,1280,768]{2,1,0:T(8,128)(2,1)} fusion(bf16[1,3072,768]{2,1,0:T(8,128)(2,1)} %all-gather.14.cloned.1.call-done, f32[1280,3072]{1,0:T(8,128)} %fusion.34), kind=kOutput, calls=%fused_computation.88 | convolution fusion | flops 6076170240 | bytes 22413312 | tf_op jit(solution)/shard_map/dot_general | solution.py:129
  412.6 74.5 %all-gather.18.cloned.1.call-done = bf16[1,3072,768]{2,1,0:T(8,128)(2,1)} async-done(((bf16[1,768,768]{2,1,0:T(8,128)(2,1)}), bf16[1,3072,768]{2,1,0:T(8,128)(2,1)}) %all-gather.18.cloned.1.call-update) | async-done | bytes 4718608 | tf_op jit(solution)/shard_map/all_gather | solution.py:185
  487.0 14.4 %fusion.74 = bf16[1,1280,768]{2,1,0:T(8,128)(2,1)S(1)} fusion(bf16[1,3072,768]{2,1,0:T(8,128)(2,1)} %all-gather.18.cloned.1.call-done, f32[1280,3072]{1,0:T(8,128)} %fusion.28), kind=kOutput, calls=%fused_computation.89 | convolution fusion | flops 6076170240 | bytes 22413312 | tf_op jit(solution)/shard_map/dot_general | solution.py:129
  501.9 15.4 %copy.68 = bf16[2,1280,768]{2,0,1:T(2,128)(2,1)} copy(bf16[2,1280,768]{2,1,0:T(8,128)(2,1)S(1)} %pad_maximum_fusion.1) | data formatting | bytes 7864320 | tf_op jit(solution)/shard_map/stack | solution.py:250
  522.0 68.1 %all-gather = bf16[32,24,16]{1,2,0:T(8,128)(2,1)S(1)} all-gather(bf16[1,24,16]{1,2,0:T(8,128)(2,1)S(1)} %bitcast.142), channel_id=1, replica_groups=mesh['wide'=8,'narrow'=4] {'wide','narrow'}, dimensions={0}, use_global_device_ids=true | all-gather | bytes 25344 | tf_op jit(solution)/shard_map/all_gather | solution.py:179
  595.0 8.5 mul.296
  608.9 11.1 gather_fusion.2
  631.6 8.6 gather_fusion.1
  642.7 48.7 %all_to_all.60 = bf16[16,160,768]{2,1,0:T(8,128)(2,1)S(1)} all-to-all(bf16[16,160,768]{2,1,0:T(8,128)(2,1)S(1)} %broadcast_select_fusion), channel_id=1, replica_groups=mesh['wide'=8,'narrow'=4] {'wide'}, dimensions={0} | all-to-all | bytes 7864320 | tf_op jit(solution)/shard_map/all_to_all | solution.py:251
  694.3 13.1 %fusion.37 = bf16[1,3072,768]{2,1,0:T(8,128)(2,1)} fusion(bf16[1280,768]{1,0:T(8,128)(2,1)S(1)} %bitcast.134, f32[1280,3072]{1,0:T(8,128)} %fusion.28), kind=kOutput, calls=%fused_computation.56 | convolution fusion | flops 6077546496 | bytes 22413312 | tf_op jit(solution)/shard_map/dot_general | solution.py:143
  707.5 19.8 %fusion.13 = bf16[1280,3072]{1,0:T(8,128)(2,1)S(1)} fusion(f32[1280,3072]{1,0:T(8,128)} %fusion.28, bf16[1280,768]{1,0:T(8,128)(2,1)} %bitcast.135, bf16[1,3072,768]{2,1,0:T(8,128)(2,1)} %all-gather.18.cloned.1.call-done), kind=kOutput, calls=%fused_computation.22 | convolution fusion | flops 6118440960 | bytes 30277632 | tf_op jit(solution)/shard_map/dot_general | solution.py:136
  739.9 23.5 %fusion.66 = bf16[1,1280,768]{2,1,0:T(8,128)(2,1)} fusion(bf16[1,768,3072]{2,1,0:T(8,128)(2,1)} %all-gather.12.cloned.1.call-done, f32[1280,3072]{1,0:T(8,128)} %fusion.34, bf16[1280,768]{1,0:T(8,128)(2,1)S(1)} %bitcast.133, bf16[1,3072,768]{2,1,0:T(8,128)(2,1)} %all-gather.14.cloned.1.call-done), kind=kOutput, calls=%fused_computation.87 | convolution fusion | flops 12159221760 | bytes 29097984 | tf_op jit(solution)/shard_map/dot_general | solution.py:149
  763.4 10.2 fusion.77
  774.0 15.4 %copy.71 = bf16[2,1280,768]{2,0,1:T(2,128)(2,1)} copy(bf16[2,1280,768]{2,1,0:T(8,128)(2,1)S(1)} %pad_maximum_fusion.2) | data formatting | bytes 7864320 | tf_op jit(solution)/shard_map/stack | solution.py:269
  794.2 46.2 %all-to-all-done.3 = bf16[2,1280,768]{2,0,1:T(2,128)(2,1)} async-done(((bf16[2,1280,768]{2,0,1:T(2,128)(2,1)}), bf16[2,1280,768]{2,0,1:T(2,128)(2,1)}, u32[]{:S(2)}, u32[]{:S(2)}) %all-to-all-start.3) | async-done | bytes 3932192 | tf_op jit(solution)/shard_map/all_to_all | solution.py:268
  845.1 13.0 %gather_fusion.3 = bf16[2048,768]{1,0:T(8,128)(2,1)} fusion(bf16[2560,768]{1,0:T(8,128)(2,1)} %bitcast.126, s32[2048]{0:T(1024)S(1)} %broadcast_clamp_fusion), kind=kCustom, calls=%fused_computation.1.clone | custom fusion | bytes 6299648 | tf_op jit(solution)/shard_map/jit(_take)/gather | solution.py:275
  881.1 12.1 %reduce_sum.193 = f32[1024,768]{1,0:T(8,128)} reduce(f32[1024,2,768]{2,1,0:T(2,128)} %reshape.189, f32[]{:T(128)} %constant.91.clone.1), dimensions={1}, to_apply=%region_12.14 | reduce | flops 786432 | bytes 9437188 | tf_op jit(solution)/shard_map/reduce_sum | solution.py:276
  897.1 29.8 %multiply_reduce_fusion.1 = f32[1024,768]{1,0:T(8,128)S(1)} fusion(f32[1024,2,768]{2,1,0:T(2,128)S(1)} %copy-done.4, f32[1024,2]{1,0:T(8,128)S(1)} %copy-done.14), kind=kLoop, calls=%fused_computation.35 | loop fusion | flops 2359296 | bytes 9445376 | tf_op jit(solution)/shard_map/reduce_sum | solution.py:273
  941.3 26.5 %attn_bwd.1 = bf16[3,1024,768]{2,1,0:T(8,128)(2,1)} custom-call(bf16[1024,2304]{1,0:T(8,128)(2,1)} %convolution_convert_fusion.q_ref.k_ref.v_ref, bf16[1024,2304]{1,0:T(8,128)(2,1)} %convolution_convert_fusion.q_ref.k_ref.v_ref, bf16[1024,2304]{1,0:T(8,128)(2,1)} %convolution_convert_fusion.q_ref.k_ref.v_ref, ...), custom_call_target="tpu_custom_call" | custom-call | tf_op jit(solution)/shard_map/attn_bwd/pallas_call | solution.py:113
  981.8 8.5 fusion.64
  990.3 38.1 %all-reduce.11 = (f32[768]{0:T(1024)S(1)}, f32[768]{0:T(1024)S(1)}, f32[768]{0:T(1024)S(1)}, f32[768]{0:T(1024)S(1)}, f32[768,16]{0,1:T(8,128)S(1)}) all-reduce(f32[768]{0:T(1024)S(1)} %get-tuple-element.18, f32[768]{0:T(1024)S(1)} %get-tuple-element.23, ...), channel_id=2, replica_groups=mesh['wide'=8,'narrow'=4] {'wide','narrow'}, use_global_device_ids=true, to_apply=%region_21.23.clone | all-reduce | flops 15360 | bytes 122880
  1041.7 112.9 %reduce-scatter.6.cloned.1.call-done = f32[24,2304]{1,0:T(8,128)} async-done(((f32[768,2304]{1,0:T(8,128)}), f32[24,2304]{1,0:T(8,128)}) %reduce-scatter.6.cloned.1.call-update) | async-done | bytes 221200 | tf_op jit(solution)/shard_map/reduce_scatter | solution.py:323
  (226 shorter events, 173.1 us)
Async XLA Ops:
  7.2 66.3 %all-gather.8.cloned.1.call-start = ((), (), s32[]{:S(2)}) async-start(), calls=%async_computation.8 | async-start | bytes 3649536 | tf_op jit(solution)/shard_map/all_gather | solution.py:175
  7.9 121.4 %all-gather.10.cloned.1.call-start = ((), (), s32[]{:S(2)}) async-start(), calls=%async_computation.9 | async-start | bytes 1216512 | tf_op jit(solution)/shard_map/all_gather | solution.py:176
  8.7 60.3 %copy-start.7 = (bf16[1024,768]{1,0:T(8,128)(2,1)S(1)}, bf16[1024,768]{1,0:T(8,128)(2,1)}, u32[]{:S(2)}) copy-start(bf16[1024,768]{1,0:T(8,128)(2,1)} %param.17) | copy-start | bytes 4718596
  8.7 210.6 %all-gather.12.cloned.1.call-start = ((), (), s32[]{:S(2)}) async-start(), calls=%async_computation.10 | async-start | bytes 5898240 | tf_op jit(solution)/shard_map/all_gather | solution.py:182
  9.5 299.1 %all-gather.16.cloned.1.call-start = ((), (), s32[]{:S(2)}) async-start(), calls=%async_computation.12 | async-start | bytes 5898240 | tf_op jit(solution)/shard_map/all_gather | solution.py:184
  10.0 387.7 %all-gather.14.cloned.1.call-start = ((), (), s32[]{:S(2)}) async-start(), calls=%async_computation.11 | async-start | bytes 5898240 | tf_op jit(solution)/shard_map/all_gather | solution.py:183
  60.6 20.8 %copy-start.43 = (f32[768]{0:T(1024)}, f32[768]{0:T(1024)S(1)}, u32[]{:S(2)}) copy-start(f32[768]{0:T(1024)S(1)} %convert_element_type.106) | copy-start | bytes 9220
  60.6 20.8 %copy-start.38 = (f32[768]{0:T(1024)}, f32[768]{0:T(1024)S(1)}, u32[]{:S(2)}) copy-start(f32[768]{0:T(1024)S(1)} %convert_element_type.105) | copy-start | bytes 9220
  60.6 72.6 %copy-start.30 = (f32[768]{0:T(1024)}, f32[768]{0:T(1024)S(1)}, u32[]{:S(2)}) copy-start(f32[768]{0:T(1024)S(1)} %convert_element_type.109) | copy-start | bytes 9220
  69.3 12.1 %copy-start.34 = (f32[1024]{0:T(1024)}, f32[1024]{0:T(1024)S(1)}, u32[]{:S(2)}) copy-start(f32[1024]{0:T(1024)S(1)} %broadcast_multiply_fusion.6) | copy-start | bytes 12292
  134.8 468.8 %copy-start.5 = (bf16[1024,768]{1,0:T(8,128)(2,1)}, bf16[1024,768]{1,0:T(8,128)(2,1)S(1)}, u32[]{:S(2)}) copy-start(bf16[1024,768]{1,0:T(8,128)(2,1)S(1)} %add_convert_fusion.1) | copy-start | bytes 4718596
  147.2 50.8 %all-to-all-start = ((bf16[16,160,768]{2,1,0:T(8,128)(2,1)}), bf16[16,160,768]{2,1,0:T(8,128)(2,1)}, u32[]{:S(2)}, u32[]{:S(2)}) async-start(bf16[16,160,768]{2,1,0:T(8,128)(2,1)} %broadcast_select_fusion.1), calls=%async_computation | async-start | bytes 7864320 | tf_op jit(solution)/shard_map/all_to_all | solution.py:247
  151.7 335.3 %all-gather.18.cloned.1.call-start = ((), (), s32[]{:S(2)}) async-start(), calls=%async_computation.13 | async-start | bytes 5898240 | tf_op jit(solution)/shard_map/all_gather | solution.py:185
  487.0 14.4 %copy-start.19 = (bf16[1,1280,768]{2,1,0:T(8,128)(2,1)S(1)}, bf16[1,1280,768]{2,1,0:T(8,128)(2,1)}, u32[]{:S(2)}) copy-start(bf16[1,1280,768]{2,1,0:T(8,128)(2,1)} %fusion.71) | copy-start | bytes 5898244
  517.3 73.1 %copy-start.11 = (bf16[1024,768]{1,0:T(8,128)(2,1)S(1)}, bf16[1024,768]{1,0:T(8,128)(2,1)}, u32[]{:S(2)}) copy-start(bf16[1024,768]{1,0:T(8,128)(2,1)} %param.18) | copy-start | bytes 4718596
  517.3 86.9 %all-to-all-start.1 = ((bf16[2,1280,768]{2,0,1:T(2,128)(2,1)}), bf16[2,1280,768]{2,0,1:T(2,128)(2,1)}, u32[]{:S(2)}, u32[]{:S(2)}) async-start(bf16[2,1280,768]{2,0,1:T(2,128)(2,1)} %copy.68), calls=%async_computation.1 | async-start | bytes 7864320 | tf_op jit(solution)/shard_map/all_to_all | solution.py:250
  522.0 514.0 %reduce-scatter.12.cloned.1.call-start = ((), (), s32[]{:S(2)}) async-start(), calls=%async_computation.17 | async-start | bytes 5898240 | tf_op jit(solution)/shard_map/reduce_scatter | solution.py:316
  590.3 13.2 %copy-start.24 = (bf16[768,16]{0,1:T(8,128)(2,1)}, bf16[768,16]{0,1:T(8,128)(2,1)S(1)}, u32[]{:S(2)}) copy-start(bf16[768,16]{0,1:T(8,128)(2,1)S(1)} %reshape.243) | copy-start | bytes 73732
  603.5 16.4 %copy-start.36 = (pred[2048]{0:T(1024)(128)(4,1)}, pred[2048]{0:T(1024)(128)(4,1)S(1)}, u32[]{:S(2)}) copy-start(pred[2048]{0:T(1024)(128)(4,1)S(1)} %compare_and_fusion.2) | copy-start | bytes 6148
  707.4 23.0 %copy-start.15 = (bf16[1,8,160,768]{3,2,0,1:T(8,128)(2,1)S(1)}, bf16[1,8,160,768]{3,2,0,1:T(8,128)(2,1)}, u32[]{:S(2)}) copy-start(bf16[1,8,160,768]{3,2,0,1:T(8,128)(2,1)} %get-tuple-element.45) | copy-start | bytes 5898244
  707.4 331.4 %reduce-scatter.10.cloned.1.call-start = ((), (), s32[]{:S(2)}) async-start(), calls=%async_computation.16 | async-start | bytes 5898240 | tf_op jit(solution)/shard_map/reduce_scatter | solution.py:313
  789.4 50.9 %all-to-all-start.3 = ((bf16[2,1280,768]{2,0,1:T(2,128)(2,1)}), bf16[2,1280,768]{2,0,1:T(2,128)(2,1)}, u32[]{:S(2)}, u32[]{:S(2)}) async-start(bf16[2,1280,768]{2,0,1:T(2,128)(2,1)} %copy.71), calls=%async_computation.3 | async-start | bytes 7864320 | tf_op jit(solution)/shard_map/all_to_all | solution.py:268
  794.1 247.7 %reduce-scatter.8.cloned.1.call-start = ((), (), s32[]{:S(2)}) async-start(), calls=%async_computation.15 | async-start | bytes 2433024 | tf_op jit(solution)/shard_map/reduce_scatter | solution.py:324
  845.1 13.1 %copy-start.3 = (bf16[2048,768]{1,0:T(8,128)(2,1)S(1)}, bf16[2048,768]{1,0:T(8,128)(2,1)}, u32[]{:S(2)}) copy-start(bf16[2048,768]{1,0:T(8,128)(2,1)} %copy-done.2) | copy-start | bytes 9437188
  845.1 13.1 %copy-start.37 = (pred[2048]{0:T(1024)(128)(4,1)S(1)}, pred[2048]{0:T(1024)(128)(4,1)}, u32[]{:S(2)}) copy-start(pred[2048]{0:T(1024)(128)(4,1)} %copy-done.36) | copy-start | bytes 6148
  881.0 12.2 %copy-start.1 = (f32[1024,768]{1,0:T(8,128)S(1)}, f32[1024,768]{1,0:T(8,128)}, u32[]{:S(2)}) copy-start(f32[1024,768]{1,0:T(8,128)} %copy-done) | copy-start | bytes 9437188
  881.0 12.2 %copy-start.25 = (bf16[768,16]{0,1:T(8,128)(2,1)S(1)}, bf16[768,16]{0,1:T(8,128)(2,1)}, u32[]{:S(2)}) copy-start(bf16[768,16]{0,1:T(8,128)(2,1)} %copy-done.24) | copy-start | bytes 73732
  881.0 12.2 %copy-start.29 = (f32[1024]{0:T(1024)S(1)}, f32[1024]{0:T(1024)}, u32[]{:S(2)}) copy-start(f32[1024]{0:T(1024)} %copy-done.28) | copy-start | bytes 12292
  881.0 12.2 %copy-start.31 = (f32[768]{0:T(1024)S(1)}, f32[768]{0:T(1024)}, u32[]{:S(2)}) copy-start(f32[768]{0:T(1024)} %copy-done.30) | copy-start | bytes 9220
  881.0 12.2 %copy-start.33 = (f32[1024]{0:T(1024)S(1)}, f32[1024]{0:T(1024)}, u32[]{:S(2)}) copy-start(f32[1024]{0:T(1024)} %copy-done.32) | copy-start | bytes 12292
  897.1 29.8 %copy-start.12 = (bf16[1024,768]{1,0:T(8,128)(2,1)S(1)}, bf16[1024,768]{1,0:T(8,128)(2,1)}, u32[]{:S(2)}) copy-start(bf16[1024,768]{1,0:T(8,128)(2,1)} %param.18) | copy-start | bytes 4718596
  933.8 220.8 %reduce-scatter.6.cloned.1.call-start = ((), (), s32[]{:S(2)}) async-start(), calls=%async_computation.14 | async-start | bytes 7299072 | tf_op jit(solution)/shard_map/reduce_scatter | solution.py:323
  (32 other events, 140.7 us)
Sparse Core Ops, SparseCore 0:
  10.8 62.6 all-gather.7
  76.3 53.0 all-gather.9
  130.9 88.3 all-gather.11
  220.7 87.7 all-gather.15
  309.9 87.7 all-gather.13
  399.2 87.7 all-gather.17
  707.5 81.5 reduce-scatter.11
  791.5 85.7 reduce-scatter.9
  933.9 95.9 reduce-scatter.7
  1036.0 118.5 reduce-scatter.5
